TPU v7x, 128 devices: a whole 4x4x4 slice. The times are simulated.
128 devices in a mesh: dp: 4 (over z_hi, core), ctx: 32 (over z_lo, y, x).
Axes of the slice: x: 4, y: 4, z: 4 (z_hi: 2, z_lo: 2; z = z_hi * 2 + z_lo), core: 2. Of those that a mesh axis runs over, the one named last changes fastest.
Arguments:
- queries: bfloat16 [4, 4096, 4096], P('dp', 'ctx'), may hold values from -41 to 41
- attn_keys: bfloat16 [4, 4096, 4096], P('dp', 'ctx'), may hold values from -6 to 6
- attn_values: bfloat16 [4, 4096, 4096], P('dp', 'ctx'), may hold values from -6 to 6
- outer_gate: bfloat16 [4, 4096, 4096], P('dp', 'ctx'), may hold values from -6 to 6
- inner_gate: bfloat16 [4, 4096, 4096], P('dp', 'ctx'), may hold values from -6 to 6
- conv_filter: bfloat16 [256, 128], replicated, may hold values from -0.5 to 0.5
- grad_mixed: bfloat16 [4, 4096, 4096], P('dp', 'ctx'), may hold values from -6 to 6
Outputs:
- block_out: bfloat16 [4, 4096, 4096], P('dp', 'ctx')
- grad_queries: bfloat16 [4, 4096, 4096], P('dp', 'ctx')
- grad_keys: bfloat16 [4, 4096, 4096], P('dp', 'ctx')
- grad_values: bfloat16 [4, 4096, 4096], P('dp', 'ctx')
- grad_outer: bfloat16 [4, 4096, 4096], P('dp', 'ctx')
- grad_inner: bfloat16 [4, 4096, 4096], P('dp', 'ctx')
- grad_filter: float32 [256, 128], replicated
All inputs are finite; a program needn't handle non-finite values.
Results may differ from a plain program's by a relative error of at most 0.007.
Values may be sent and summed in bfloat16 or wider, within the bound.
A program may use at most 192 MiB of HBM per device.

v0:
```python
import jax
import jax.numpy as jnp
from jax import lax
from jax.sharding import PartitionSpec as P

HEAD_DIM = 128


def passed_along(value, axis, steps):
    count = lax.axis_size(axis)
    initial, last = (max(0, -steps), min(count, count - steps))
    return lax.ppermute(value, axis, [(source, source + steps) for source in range(initial, last)])


def as_sent(x):
    return jax.tree.map(lambda a: a.astype(jnp.bfloat16) if a.dtype == jnp.float32 else a, x)


def head_major(array, head_count):
    batch_size, length, channels = array.shape
    shaped = array.reshape(batch_size, length, head_count, channels // head_count)
    return shaped.transpose(0, 2, 1, 3).reshape(
        batch_size * head_count, length, channels // head_count
    )


def token_major(array, batch_size):
    heads_all, length, width = array.shape
    head_count = heads_all // batch_size
    shaped = array.reshape(batch_size, head_count, length, width)
    return shaped.transpose(0, 2, 1, 3).reshape(batch_size, length, head_count * width)


def head_both(query_rows, key_rows, value_rows, grad_rows):
    length, width = query_rows.shape
    softmax_scale = width ** (-0.5)
    block_rows = min(512, length)
    grad_k = jnp.zeros((length, width), jnp.float32)
    grad_v = jnp.zeros((length, width), jnp.float32)
    outputs, grad_q = ([], [])
    for block_id in range(length // block_rows):
        first_row = block_id * block_rows
        last_row = first_row + block_rows
        query_block = query_rows[first_row:last_row]
        scores = (
            jnp.einsum(
                "qd,kd->qk", query_block, key_rows[:last_row], preferred_element_type=jnp.float32
            )
            * softmax_scale
        )
        row_ids = first_row + jnp.arange(block_rows)[:, None]
        col_ids = jnp.arange(last_row)[None, :]
        scores = jnp.where(col_ids <= row_ids, scores, -jnp.inf)
        row_max = jnp.max(scores, axis=1, keepdims=True)
        row_total = jnp.sum(jnp.exp(scores - row_max), axis=1, keepdims=True)
        attn_probs = jnp.exp(scores - row_max) / row_total
        probs_low = attn_probs.astype(jnp.bfloat16)
        outputs.append(
            jnp.dot(probs_low, value_rows[:last_row], preferred_element_type=jnp.float32).astype(
                jnp.bfloat16
            )
        )
        grad_block = grad_rows[first_row:last_row]
        grad_probs = jnp.einsum(
            "qd,kd->qk", grad_block, value_rows[:last_row], preferred_element_type=jnp.float32
        )
        row_inner = jnp.sum(attn_probs * grad_probs, axis=1, keepdims=True)
        grad_scores = (attn_probs * (grad_probs - row_inner)).astype(jnp.bfloat16)
        grad_q.append(
            (
                jnp.dot(grad_scores, key_rows[:last_row], preferred_element_type=jnp.float32)
                * softmax_scale
            ).astype(jnp.bfloat16)
        )
        grad_k = grad_k.at[:last_row].add(
            jnp.einsum("qk,qd->kd", grad_scores, query_block, preferred_element_type=jnp.float32)
        )
        grad_v = grad_v.at[:last_row].add(
            jnp.einsum("qk,qd->kd", probs_low, grad_block, preferred_element_type=jnp.float32)
        )
    return (
        jnp.concatenate(outputs, axis=0),
        jnp.concatenate(grad_q, axis=0),
        (grad_k * softmax_scale).astype(jnp.bfloat16),
        grad_v.astype(jnp.bfloat16),
    )


def depthwise(signal, taps):
    return lax.conv_general_dilated(
        signal,
        taps[:, None, :],
        (1,),
        "VALID",
        dimension_numbers=("NWC", "WIO", "NWC"),
        feature_group_count=signal.shape[2],
        preferred_element_type=jnp.float32,
    )


def channel_taps(filter_rows, group_width):
    return jnp.repeat(filter_rows, group_width, axis=0).T


def filter_grad(grad_rows, extended, group_width, width):
    batch_size, local_rows, channels = grad_rows.shape
    signal = extended.transpose(1, 0, 2).reshape(1, extended.shape[1], batch_size * channels)
    kernel_rows = grad_rows.transpose(1, 0, 2).reshape(local_rows, batch_size * channels)
    result = depthwise(signal, kernel_rows)[0]
    per_channel = result.reshape(width, batch_size, channels).sum(axis=1)[::-1]
    return per_channel.T.reshape(channels // group_width, group_width, width).sum(axis=1)


def on_device(queries, attn_keys, attn_values, outer_gate, inner_gate, conv_filter, grad_mixed):
    batch_size, local_rows, channel_count = queries.shape
    ctx_size = lax.axis_size("ctx")
    local_ch = channel_count // ctx_size
    heads_here = local_ch // HEAD_DIM
    seq_len = local_rows * ctx_size
    group_total, width = conv_filter.shape
    group_width = channel_count // group_total

    def to_heads(array):
        return array.reshape(batch_size, local_rows, ctx_size, local_ch)

    def to_tokens(array):
        return array.reshape(batch_size, seq_len, 1, local_ch)

    def from_heads(array):
        return array.reshape(batch_size, seq_len, local_ch)

    def from_tokens(array):
        return array.reshape(batch_size, local_rows, channel_count)

    taps_all = channel_taps(conv_filter, group_width)
    grad_filtered = (grad_mixed.astype(jnp.float32) * outer_gate.astype(jnp.float32)).astype(
        jnp.bfloat16
    )
    after_rows = passed_along(grad_filtered[:, : width - 1], "ctx", -1)
    grad_gated = depthwise(jnp.concatenate([grad_filtered, after_rows], axis=1), taps_all)
    grad_attended = (grad_gated * inner_gate.astype(jnp.float32)).astype(jnp.bfloat16)
    received = (
        lax.all_to_all(to_heads(queries), "ctx", split_axis=2, concat_axis=1, tiled=True),
        lax.all_to_all(to_heads(attn_keys), "ctx", split_axis=2, concat_axis=1, tiled=True),
        lax.all_to_all(to_heads(attn_values), "ctx", split_axis=2, concat_axis=1, tiled=True),
        lax.all_to_all(to_heads(grad_attended), "ctx", split_axis=2, concat_axis=1, tiled=True),
    )
    attn_heads, grad_qh, grad_kh, grad_vh = jax.vmap(head_both)(
        head_major(from_heads(received[0]), heads_here),
        head_major(from_heads(received[1]), heads_here),
        head_major(from_heads(received[2]), heads_here),
        head_major(from_heads(received[3]), heads_here),
    )
    sent_back = (
        lax.all_to_all(
            as_sent(to_tokens(token_major(attn_heads, batch_size))),
            "ctx",
            split_axis=1,
            concat_axis=2,
            tiled=True,
        ),
        lax.all_to_all(
            as_sent(to_tokens(token_major(grad_qh, batch_size))),
            "ctx",
            split_axis=1,
            concat_axis=2,
            tiled=True,
        ),
        lax.all_to_all(
            as_sent(to_tokens(token_major(grad_kh, batch_size))),
            "ctx",
            split_axis=1,
            concat_axis=2,
            tiled=True,
        ),
        lax.all_to_all(
            as_sent(to_tokens(token_major(grad_vh, batch_size))),
            "ctx",
            split_axis=1,
            concat_axis=2,
            tiled=True,
        ),
    )
    attended, grad_queries, grad_keys, grad_values = [from_tokens(array) for array in sent_back]
    gated_in = (inner_gate.astype(jnp.float32) * attended.astype(jnp.float32)).astype(jnp.bfloat16)
    rim_rows = passed_along(gated_in[:, local_rows - (width - 1) :], "ctx", 1)
    extended = jnp.concatenate([rim_rows, gated_in], axis=1)
    filtered = depthwise(extended, taps_all[::-1])
    block_out = (outer_gate.astype(jnp.float32) * filtered).astype(jnp.bfloat16)
    grad_outer = (grad_mixed.astype(jnp.float32) * filtered).astype(jnp.bfloat16)
    partial_grad = filter_grad(grad_filtered, extended, group_width, width)
    grad_inner = (grad_gated * attended.astype(jnp.float32)).astype(jnp.bfloat16)
    grad_filter = lax.psum(partial_grad, ("dp", "ctx"))
    return (block_out, grad_queries, grad_keys, grad_values, grad_outer, grad_inner, grad_filter)


def solution(mesh):
    return jax.shard_map(
        on_device,
        mesh=mesh,
        in_specs=(
            P("dp", "ctx", None),
            P("dp", "ctx", None),
            P("dp", "ctx", None),
            P("dp", "ctx", None),
            P("dp", "ctx", None),
            P(),
            P("dp", "ctx", None),
        ),
        out_specs=(
            P("dp", "ctx", None),
            P("dp", "ctx", None),
            P("dp", "ctx", None),
            P("dp", "ctx", None),
            P("dp", "ctx", None),
            P("dp", "ctx", None),
            P(),
        ),
        check_vma=False,
    )
```

profile of v0, /device:TPU:1, one launch (start us, length us, event | category | flops | bytes accessed | tf_op | source)
XLA Modules:
  0.0 730.8 jit_solution(2601771301211518141)
XLA Ops:
  9.5 9.3 %all-to-all-start = ((bf16[1,128,32,128]{1,3,0,2:T(8,128)(2,1)}), bf16[1,128,32,128]{1,3,0,2:T(8,128)(2,1)S(1)}, u32[]{:S(2)}, u32[]{:S(2)}) async-start(bf16[1,128,32,128]{1,3,0,2:T(8,128)(2,1)} %bitcast.1), calls=%async_computation | async-start | bytes 2097152 | tf_op jit(solution)/shard_map/all_to_all | solution.py:143
  20.2 14.3 %all-to-all-done = bf16[1,128,32,128]{1,3,0,2:T(8,128)(2,1)S(1)} async-done(((bf16[1,128,32,128]{1,3,0,2:T(8,128)(2,1)}), bf16[1,128,32,128]{1,3,0,2:T(8,128)(2,1)S(1)}, u32[]{:S(2)}, u32[]{:S(2)}) %all-to-all-start) | async-done | bytes 1048608 | tf_op jit(solution)/shard_map/all_to_all | solution.py:143
  34.5 4.2 all-to-all-start.1
  38.7 7.8 %multiply_convert_fusion.10 = bf16[1,128,4096]{2,0,1:T(2,128)(2,1)S(1)} fusion(bf16[1,128,4096]{2,1,0:T(8,128)(2,1)} %param.46, bf16[1,128,4096]{2,1,0:T(8,128)(2,1)S(1)} %copy-done.27), kind=kLoop, calls=%fused_computation.99 | loop fusion | flops 2097152 | bytes 3145728 | tf_op jit(solution)/shard_map/convert_element_type | solution.py:136
  55.2 4.3 copy.151
  61.9 4.2 copy.156
  66.9 9.7 %all-to-all-start.2 = ((bf16[1,128,32,128]{1,3,0,2:T(8,128)(2,1)}), bf16[1,128,32,128]{1,3,0,2:T(8,128)(2,1)}, u32[]{:S(2)}, u32[]{:S(2)}) async-start(bf16[1,128,32,128]{1,3,0,2:T(8,128)(2,1)} %bitcast.13), calls=%async_computation.2 | async-start | bytes 2097152 | tf_op jit(solution)/shard_map/all_to_all | solution.py:145
  84.9 3.3 fusion.171
  89.7 4.5 fusion.172
  94.2 4.3 fusion.173
  121.8 3.6 copy.154
  125.4 35.9 %multiply_convert_fusion.9 = (bf16[1,128,4096]{2,0,1:T(2,128)(2,1)S(1)}, f32[1,128,4096]{2,0,1:T(1,128)}) fusion(bf16[1,128,4096]{2,1,0:T(8,128)(2,1)S(1)} %copy-done.34, bf16[128,1,4096]{2,1,0:T(2,128)(2,1)S(1)} %copy-done.31, bf16[1,127,4096]{2,0,1:T(2,128)(2,1)S(1)} %copy.154, bf16[1,128,4096]{2,0,1:T(2,128)(2,1)S(1)} %copy-done.15), kind=kOutput, calls=%fused_computation.98 | convolution fusion | flops 139968512 | bytes 7331840 | tf_op jit(solution)/shard_map/conv_general_dilated | solution.py:90
  161.3 3.6 copy.157
  164.9 7.9 %all-to-all-start.4 = ((bf16[1,128,32,128]{1,3,0,2:T(8,128)(2,1)}), bf16[1,128,32,128]{1,3,0,2:T(8,128)(2,1)S(1)}, u32[]{:S(2)}, u32[]{:S(2)}) async-start(bf16[1,128,32,128]{1,3,0,2:T(8,128)(2,1)} %bitcast.63), calls=%async_computation.4 | async-start | bytes 2097152 | tf_op jit(solution)/shard_map/all_to_all | solution.py:146
  172.8 3.8 fusion.5
  176.6 4.7 fusion.98
  181.3 4.5 all-to-all-done.4
  229.9 4.0 multiply_reduce_fusion.1
  236.8 7.0 multiply_convert_fusion.1
  246.5 7.3 %multiply_reduce_fusion = (f32[512]{0:T(512)S(1)}, f32[512,4096]{1,0:T(8,128)S(1)}, f32[512,4096]{1,0:T(8,128)}) fusion(f32[512]{0:T(512)S(1)} %copy-done.70, f32[512,4096]{1,0:T(8,128)} %copy-done.10, f32[512]{0:T(512)S(1)} %copy-done.69, bf16[4096,128]{1,0:T(8,128)(2,1)S(1)} %bitcast.481, bf16[1,4096,128]{2,1,0:T(8,128)(2,1)S(1)} %bitcast.538), kind=kOutput, calls=%fused_computation.1 | convolution fusion | flops 545259008 | bytes 26351616 | tf_op jit(solution)/shard_map/vmap(qd,kd->qk)/dot_general | solution.py:64
  257.2 7.9 %multiply_convert_fusion = bf16[512,4096]{1,0:T(8,128)(2,1)S(1)} fusion(f32[512,4096]{1,0:T(8,128)} %copy-done, f32[512,4096]{1,0:T(8,128)} %get-tuple-element.284, f32[512]{0:T(512)S(1)} %get-tuple-element.257), kind=kLoop, calls=%fused_computation | loop fusion | flops 6291456 | bytes 20973568 | tf_op jit(solution)/shard_map/vmap()/convert_element_type | solution.py:68
  265.2 3.3 fusion.15
  269.8 16.7 %copy.219 = bf16[1,4096,1,128]{3,2,0,1:T(2,128)(2,1)S(1)} copy(bf16[1,4096,1,128]{3,1,2,0:T(8,128)(2,1)S(1)} %bitcast.539) | data formatting | bytes 2097152 | tf_op jit(solution)/shard_map/transpose;reshape | solution.py:31
  287.1 23.4 %reduce.81 = bf16[4096,128]{1,0:T(8,128)(2,1)} reduce(bf16[4096,1,1,128]{3,2,1,0:T(2,128)(2,1)S(1)} %bitcast.486, bf16[]{:T(256)} %broadcast.399), dimensions={1,2}, to_apply=%bitcast.455.reduce_sub_computation | reduce | bytes 2097154
  312.6 16.7 %copy.218 = bf16[1,4096,1,128]{3,2,0,1:T(2,128)(2,1)S(1)} copy(bf16[1,4096,1,128]{3,1,2,0:T(8,128)(2,1)S(1)} %copy-done.21) | data formatting | bytes 2097152 | tf_op jit(solution)/shard_map/transpose;reshape | solution.py:31
  329.2 22.6 %reduce.82 = bf16[4096,128]{1,0:T(8,128)(2,1)S(1)} reduce(bf16[4096,1,1,128]{3,2,1,0:T(2,128)(2,1)S(1)} %bitcast.488, bf16[]{:T(256)} %broadcast.399), dimensions={1,2}, to_apply=%bitcast.454.reduce_sub_computation | reduce | bytes 2097154
  356.1 22.4 %reduce.80 = bf16[4096,128]{1,0:T(8,128)(2,1)S(1)} reduce(bf16[4096,1,1,128]{3,2,1,0:T(2,128)(2,1)S(1)} %bitcast.489, bf16[]{:T(256)} %broadcast.399), dimensions={1,2}, to_apply=%bitcast.456.reduce_sub_computation | reduce | bytes 2097154
  379.6 5.3 all-to-all-start.3
  385.0 6.1 fusion.32
  391.1 4.0 fusion.9
  396.6 6.4 all-to-all-start.5
  403.1 4.7 fusion.16
  407.8 16.7 %copy.217 = bf16[1,4096,1,128]{3,2,0,1:T(2,128)(2,1)S(1)} copy(bf16[1,4096,1,128]{3,1,2,0:T(8,128)(2,1)S(1)} %fusion.16) | data formatting | bytes 2097152 | tf_op jit(solution)/shard_map/transpose;reshape | solution.py:31
  424.5 23.4 %reduce.83 = bf16[4096,128]{1,0:T(8,128)(2,1)} reduce(bf16[4096,1,1,128]{3,2,1,0:T(2,128)(2,1)S(1)} %bitcast.487, bf16[]{:T(256)} %broadcast.399), dimensions={1,2}, to_apply=%bitcast.453.reduce_sub_computation | reduce | bytes 2097154
  450.0 4.3 reshape.1127
  457.8 8.1 %all-to-all-start.6 = ((bf16[32,2,8192]{2,1,0:T(2,128)(2,1)}), bf16[32,2,8192]{2,1,0:T(2,128)(2,1)}, u32[]{:S(2)}, u32[]{:S(2)}) async-start(bf16[32,2,8192]{2,1,0:T(2,128)(2,1)} %reshape.1130), calls=%async_computation.6 | async-start | bytes 2097152 | tf_op jit(solution)/shard_map/all_to_all | solution.py:169
  465.9 6.2 multiply_convert_fusion.6
  476.4 4.3 collective-permute-start
  480.7 6.5 all-to-all-start.7
  487.3 9.8 %fusion.202 = bf16[128,1,4096]{2,1,0:T(2,128)(2,1)} fusion(bf16[1,128,4096]{2,1,0:T(8,128)(2,1)S(1)} %copy-done.30, bf16[1,128,4096]{2,1,0:T(8,128)(2,1)S(1)} %copy-done.28), kind=kLoop, calls=%fused_computation.90.clone.2 | loop fusion | flops 2097152 | bytes 3145728 | tf_op jit(solution)/shard_map/conv_general_dilated | solution.py:90
  500.3 4.3 reshape.1131
  510.4 8.6 %all-to-all-done.7 = bf16[32,2,8192]{2,1,0:T(2,128)(2,1)} async-done(((bf16[32,2,8192]{2,1,0:T(2,128)(2,1)}), bf16[32,2,8192]{2,1,0:T(2,128)(2,1)}, u32[]{:S(2)}, u32[]{:S(2)}) %all-to-all-start.7) | async-done | bytes 1048608 | tf_op jit(solution)/shard_map/all_to_all | solution.py:176
  519.0 4.3 reshape.1133
  527.0 3.6 copy.150
  530.6 33.8 %fusion.44 = f32[1,128,4096]{2,0,1:T(1,128)S(1)} fusion(bf16[1,128,4096]{2,0,1:T(2,128)(2,1)S(1)} %copy-done.17, bf16[1,127,4096]{2,0,1:T(2,128)(2,1)S(1)} %copy.150, bf16[128,1,4096]{2,1,0:T(2,128)(2,1)} %fusion.202), kind=kOutput, calls=%fused_computation.89 | convolution fusion | flops 138395648 | bytes 5234688 | tf_op jit(solution)/shard_map/conv_general_dilated | solution.py:90
  566.1 10.4 %rev.7 = f32[128,4096]{1,0:T(8,128)} reverse(f32[128,4096]{1,0:T(8,128)S(1)} %bitcast.491), dimensions={0} | reverse | bytes 4194304 | tf_op jit(solution)/shard_map/rev | solution.py:110
  579.5 39.3 %multiply_convert_fusion.7 = (bf16[1,128,4096]{2,0,1:T(2,128)(2,1)S(1)}, bf16[1,128,4096]{2,0,1:T(2,128)(2,1)S(1)}) fusion(bf16[1,128,4096]{2,1,0:T(8,128)(2,1)S(1)} %copy-done.29, bf16[1,128,4096]{2,1,0:T(8,128)(2,1)} %param.46, bf16[128,1,4096]{2,1,0:T(2,128)(2,1)} %copy.151, bf16[1,128,4096]{2,0,1:T(2,128)(2,1)} %copy-done.16, ...), kind=kOutput, calls=%fused_computation.95 | convolution fusion | flops 141541376 | bytes 7331840 | tf_op jit(solution)/shard_map/conv_general_dilated | solution.py:90
  623.0 99.2 %all-reduce.4.cloned.1.call-done = f32[256,128]{1,0:T(8,128)} async-done(((f32[256,128]{1,0:T(8,128)}), f32[256,128]{1,0:T(8,128)}) %all-reduce.4.cloned.1.call-update) | async-done | bytes 131088 | tf_op jit(solution)/shard_map/psum | solution.py:193
  (285 shorter events, 144.7 us)
Async XLA Ops:
  7.2 11.7 %copy-start.37 = (bf16[1,128,4096]{2,1,0:T(8,128)(2,1)S(1)}, bf16[1,128,4096]{2,1,0:T(8,128)(2,1)}, u32[]{:S(2)}) copy-start(bf16[1,128,4096]{2,1,0:T(8,128)(2,1)} %param.44) | copy-start | bytes 3145732
  9.5 29.2 %copy-start.27 = (bf16[1,128,4096]{2,1,0:T(8,128)(2,1)S(1)}, bf16[1,128,4096]{2,1,0:T(8,128)(2,1)}, u32[]{:S(2)}) copy-start(bf16[1,128,4096]{2,1,0:T(8,128)(2,1)} %param.49) | copy-start | bytes 3145732
  9.5 24.9 %all-to-all-start = ((bf16[1,128,32,128]{1,3,0,2:T(8,128)(2,1)}), bf16[1,128,32,128]{1,3,0,2:T(8,128)(2,1)S(1)}, u32[]{:S(2)}, u32[]{:S(2)}) async-start(bf16[1,128,32,128]{1,3,0,2:T(8,128)(2,1)} %bitcast.1), calls=%async_computation | async-start | bytes 2097152 | tf_op jit(solution)/shard_map/all_to_all | solution.py:143
  34.5 12.0 %copy-start.25 = (bf16[1,128,32,128]{1,3,0,2:T(8,128)(2,1)}, bf16[1,128,32,128]{1,3,0,2:T(8,128)(2,1)S(1)}, u32[]{:S(2)}) copy-start(bf16[1,128,32,128]{1,3,0,2:T(8,128)(2,1)S(1)} %all-to-all-done) | copy-start | bytes 3145732
  34.5 32.4 %all-to-all-start.1 = ((bf16[1,128,32,128]{1,3,0,2:T(8,128)(2,1)}), bf16[1,128,32,128]{1,3,0,2:T(8,128)(2,1)S(1)}, u32[]{:S(2)}, u32[]{:S(2)}) async-start(bf16[1,128,32,128]{1,3,0,2:T(8,128)(2,1)} %bitcast.7), calls=%async_computation.1 | async-start | bytes 2097152 | tf_op jit(solution)/shard_map/all_to_all | solution.py:144
  46.5 5.6 copy-start.43
  50.8 70.9 %collective-permute-start.1 = (bf16[1,127,4096]{2,1,0:T(8,128)(2,1)}, bf16[1,127,4096]{2,1,0:T(8,128)(2,1)}, u32[]{:S(2)}, u32[]{:S(2)}) collective-permute-start(bf16[1,127,4096]{2,1,0:T(8,128)(2,1)} %copy.153), channel_id=1, source_target_pairs={{1,0},{2,1},{3,2},{4,3},{5,4},{6,5},{7,6},{8,7},{9,8},{10,9},{11,1... | collective-permute-start | bytes 3121160 | tf_op jit(solution)/shard_map/ppermute | solution.py:12
  59.5 6.6 copy-start.26
  66.8 10.4 %copy-start.18 = (bf16[1,128,32,128]{3,1,2,0:T(8,128)(2,1)}, bf16[1,128,32,128]{3,1,2,0:T(8,128)(2,1)S(1)}, u32[]{:S(2)}) copy-start(bf16[1,128,32,128]{3,1,2,0:T(8,128)(2,1)S(1)} %copy.140) | copy-start | bytes 3145732
  66.9 31.7 %all-to-all-start.2 = ((bf16[1,128,32,128]{1,3,0,2:T(8,128)(2,1)}), bf16[1,128,32,128]{1,3,0,2:T(8,128)(2,1)}, u32[]{:S(2)}, u32[]{:S(2)}) async-start(bf16[1,128,32,128]{1,3,0,2:T(8,128)(2,1)} %bitcast.13), calls=%async_computation.2 | async-start | bytes 2097152 | tf_op jit(solution)/shard_map/all_to_all | solution.py:145
  80.0 24.0 %copy-start.49 = (f32[512]{0:T(512)}, f32[512]{0:T(512)S(1)}, u32[]{:S(2)}) copy-start(f32[512]{0:T(512)S(1)} %get-tuple-element.267) | copy-start | bytes 6148
  82.0 23.8 %copy-start.6 = (f32[512,1536]{1,0:T(8,128)}, f32[512,1536]{1,0:T(8,128)S(1)}, u32[]{:S(2)}) copy-start(f32[512,1536]{1,0:T(8,128)S(1)} %get-tuple-element.270) | copy-start | bytes 9437188
  82.0 23.8 %copy-start.61 = (f32[512]{0:T(512)}, f32[512]{0:T(512)S(1)}, u32[]{:S(2)}) copy-start(f32[512]{0:T(512)S(1)} %get-tuple-element.269) | copy-start | bytes 6148
  84.9 23.9 %copy-start.57 = (f32[512]{0:T(512)}, f32[512]{0:T(512)S(1)}, u32[]{:S(2)}) copy-start(f32[512]{0:T(512)S(1)} %get-tuple-element.271) | copy-start | bytes 6148
  88.2 31.8 %copy-start.45 = (f32[512]{0:T(512)}, f32[512]{0:T(512)S(1)}, u32[]{:S(2)}) copy-start(f32[512]{0:T(512)S(1)} %get-tuple-element.273) | copy-start | bytes 6148
  88.5 12.5 %copy-start.53 = (f32[512]{0:T(512)}, f32[512]{0:T(512)S(1)}, u32[]{:S(2)}) copy-start(f32[512]{0:T(512)S(1)} %get-tuple-element.265) | copy-start | bytes 6148
  89.7 11.3 %copy-start.55 = (f32[512]{0:T(512)}, f32[512]{0:T(512)S(1)}, u32[]{:S(2)}) copy-start(f32[512]{0:T(512)S(1)} %fusion.136) | copy-start | bytes 6148
  98.5 11.8 %copy-start.65 = (f32[512]{0:T(512)}, f32[512]{0:T(512)S(1)}, u32[]{:S(2)}) copy-start(f32[512]{0:T(512)S(1)} %get-tuple-element.279) | copy-start | bytes 6148
  111.4 7.7 %slice-start.4 = ((s8[5242880]{0:T(1024)(128)(4,1)}), s8[4194304]{0:T(1024)(128)(4,1)S(1)}, s32[]{:S(2)}) async-start(s8[5242880]{0:T(1024)(128)(4,1)} %bitcast.461), calls=%async_computation.13 | async-start | bytes 8388608
  113.2 6.0 slice-start.5
  120.0 5.3 copy-start.15
  120.0 5.3 copy-start.31
  120.0 5.3 copy-start.34
  161.3 11.5 %copy-start.44 = (f32[512]{0:T(512)S(1)}, f32[512]{0:T(512)}, u32[]{:S(2)}) copy-start(f32[512]{0:T(512)} %get-tuple-element.275) | copy-start | bytes 6148
  164.9 21.0 %all-to-all-start.4 = ((bf16[1,128,32,128]{1,3,0,2:T(8,128)(2,1)}), bf16[1,128,32,128]{1,3,0,2:T(8,128)(2,1)S(1)}, u32[]{:S(2)}, u32[]{:S(2)}) async-start(bf16[1,128,32,128]{1,3,0,2:T(8,128)(2,1)} %bitcast.63), calls=%async_computation.4 | async-start | bytes 2097152 | tf_op jit(solution)/shard_map/all_to_all | solution.py:146
  176.6 10.5 %copy-start.24 = (f32[512,512]{0,1:T(8,128)S(1)}, f32[512,512]{0,1:T(8,128)}, u32[]{:S(2)}) copy-start(f32[512,512]{0,1:T(8,128)} %copy-done.23) | copy-start | bytes 3145732
  176.6 10.5 %copy-start.54 = (f32[512]{0:T(512)S(1)}, f32[512]{0:T(512)}, u32[]{:S(2)}) copy-start(f32[512]{0:T(512)} %copy-done.53) | copy-start | bytes 6148
  176.6 10.5 %copy-start.56 = (f32[512]{0:T(512)S(1)}, f32[512]{0:T(512)}, u32[]{:S(2)}) copy-start(f32[512]{0:T(512)} %copy-done.55) | copy-start | bytes 6148
  193.2 6.3 slice-start.6
  196.3 6.5 slice-start.2
  224.0 5.9 slice-start.10
  224.9 5.0 slice-start.11
  246.5 7.4 %copy-start.35 = (bf16[1,4096,128]{2,1,0:T(8,128)(2,1)}, bf16[1,4096,128]{2,1,0:T(8,128)(2,1)S(1)}, u32[]{:S(2)}) copy-start(bf16[1,4096,128]{2,1,0:T(8,128)(2,1)S(1)} %fusion.102) | copy-start | bytes 3145732
  286.5 26.0 %copy-start.21 = (bf16[1,4096,1,128]{3,1,2,0:T(8,128)(2,1)S(1)}, bf16[1,4096,1,128]{3,1,2,0:T(8,128)(2,1)}, u32[]{:S(2)}) copy-start(bf16[1,4096,1,128]{3,1,2,0:T(8,128)(2,1)} %fusion.15) | copy-start | bytes 3145732
  379.6 11.5 %slice-start = ((s8[7340032]{0:T(1024)(128)(4,1)}), s8[3145728]{0:T(1024)(128)(4,1)S(1)}, s32[]{:S(2)}) async-start(s8[7340032]{0:T(1024)(128)(4,1)} %bitcast.457), calls=%async_computation.9 | async-start | bytes 6291456
  379.6 17.0 %all-to-all-start.3 = ((bf16[32,2,8192]{2,1,0:T(2,128)(2,1)}), bf16[32,2,8192]{2,1,0:T(2,128)(2,1)}, u32[]{:S(2)}, u32[]{:S(2)}) async-start(bf16[32,2,8192]{2,1,0:T(2,128)(2,1)} %reshape.1126), calls=%async_computation.3 | async-start | bytes 2097152 | tf_op jit(solution)/shard_map/all_to_all | solution.py:155
  384.9 6.1 slice-start.1
  395.0 8.0 %copy-start.3 = (f32[1,4096,128]{2,1,0:T(8,128)S(1)}, f32[1,4096,128]{2,1,0:T(8,128)}, u32[]{:S(2)}) copy-start(f32[1,4096,128]{2,1,0:T(8,128)} %fusion.9) | copy-start | bytes 6291460
  396.6 61.1 %all-to-all-start.5 = ((bf16[32,2,8192]{2,1,0:T(2,128)(2,1)}), bf16[32,2,8192]{2,1,0:T(2,128)(2,1)S(1)}, u32[]{:S(2)}, u32[]{:S(2)}) async-start(bf16[32,2,8192]{2,1,0:T(2,128)(2,1)} %reshape.1128), calls=%async_computation.5 | async-start | bytes 2097152 | tf_op jit(solution)/shard_map/all_to_all | solution.py:162
  457.8 22.9 %all-to-all-start.6 = ((bf16[32,2,8192]{2,1,0:T(2,128)(2,1)}), bf16[32,2,8192]{2,1,0:T(2,128)(2,1)}, u32[]{:S(2)}, u32[]{:S(2)}) async-start(bf16[32,2,8192]{2,1,0:T(2,128)(2,1)} %reshape.1130), calls=%async_computation.6 | async-start | bytes 2097152 | tf_op jit(solution)/shard_map/all_to_all | solution.py:169
  472.1 4.3 copy-start.16
  474.2 13.0 %copy-start.28 = (bf16[1,128,4096]{2,1,0:T(8,128)(2,1)S(1)}, bf16[1,128,4096]{2,1,0:T(8,128)(2,1)}, u32[]{:S(2)}) copy-start(bf16[1,128,4096]{2,1,0:T(8,128)(2,1)} %param.49) | copy-start | bytes 3145732
  474.3 13.0 %copy-start.30 = (bf16[1,128,4096]{2,1,0:T(8,128)(2,1)S(1)}, bf16[1,128,4096]{2,1,0:T(8,128)(2,1)}, u32[]{:S(2)}) copy-start(bf16[1,128,4096]{2,1,0:T(8,128)(2,1)} %param.46) | copy-start | bytes 3145732
  476.4 50.6 %collective-permute-start = (bf16[1,127,4096]{2,1,0:T(8,128)(2,1)}, bf16[1,127,4096]{2,1,0:T(8,128)(2,1)}, u32[]{:S(2)}, u32[]{:S(2)}) collective-permute-start(bf16[1,127,4096]{2,1,0:T(8,128)(2,1)} %copy.149), channel_id=1, source_target_pairs={{0,1},{1,2},{2,3},{3,4},{4,5},{5,6},{6,7},{7,8},{8,9},{9,10},{10,1... | collective-permute-start | bytes 3121160 | tf_op jit(solution)/shard_map/ppermute | solution.py:12
  480.7 38.3 %all-to-all-start.7 = ((bf16[32,2,8192]{2,1,0:T(2,128)(2,1)}), bf16[32,2,8192]{2,1,0:T(2,128)(2,1)}, u32[]{:S(2)}, u32[]{:S(2)}) async-start(bf16[32,2,8192]{2,1,0:T(2,128)(2,1)} %reshape.1132), calls=%async_computation.7 | async-start | bytes 2097152 | tf_op jit(solution)/shard_map/all_to_all | solution.py:176
  487.2 234.9 %all-reduce.4.cloned.1.call-start = ((), (), s32[]{:S(2)}) async-start(), calls=%async_computation.8 | async-start | bytes 262144 | tf_op jit(solution)/shard_map/psum | solution.py:193
  523.4 7.2 copy-start.17
  530.6 33.8 %copy-start.32 = (bf16[1,127,4096]{2,0,1:T(2,128)(2,1)}, bf16[1,127,4096]{2,0,1:T(2,128)(2,1)S(1)}, u32[]{:S(2)}) copy-start(bf16[1,127,4096]{2,0,1:T(2,128)(2,1)S(1)} %copy.150) | copy-start | bytes 3121156
  (48 other events, 112.8 us)
Sparse Core Ops, SparseCore 0:
  579.6 142.4 all-reduce.3
where the time goes:
time: 739 us; the launch traced here: 731 us
  matrix products  211 us (29%)
  local copies, waits for them, and re-layouts  159 us (22%)
  other arithmetic  154 us (21%)
  waiting for transfers between devices  128 us (17%)
  starting transfers between devices  63.1 us (9%)
  between operations  15.7 us (2%)
    conv_general_dilated x3, matrix products, depthwise(): lax.conv_general_dilated(signal, taps[:, None, :], (1,), 'VALID', dimensi...  109 us
    psum x1, waiting for transfers between devices, on_device(): grad_filter = lax.psum(partial_grad, ('dp', 'ctx'))  99.2 us
    unnamed x11, other arithmetic  91.7 us
    another operation x4, local copies, waits for them, and re-layouts, token_major(): shaped.transpose(0, 2, 1, 3).reshape(batch_size, length, head_count * width)  53.3 us
    unnamed x193, local copies, waits for them, and re-layouts  52.8 us
    convert_element_type x8, other arithmetic, head_both(): grad_scores = (attn_probs * (grad_probs - row_inner)).astype(jnp.bfloat16)  24.2 us
    dot_general x8, matrix products, head_both(): jnp.einsum('qd,kd->qk', grad_block, value_rows[:last_row], preferred_elem...  23 us
    dot_general x8, matrix products, head_both(): jnp.einsum('qd,kd->qk', query_block, key_rows[:last_row], preferred_eleme...  21.7 us
  transfers between devices with their start and end apart: 11, of which 5 were waited for; matrix products, arithmetic and copies ran while one was open for 31% of the time, Pallas kernels for 0%

commit v1 on v0

v1 whole, which is shorter than its diff:
```python
import functools
import math

import jax
import jax.numpy as jnp
from jax import lax
from jax.experimental import pallas as pl
from jax.experimental.pallas import tpu as pltpu
from jax.sharding import PartitionSpec as P

F32 = jnp.float32
BF16 = jnp.bfloat16
MESH = pl.DeviceIdType.MESH
LANES = 128
QUERY_BLOCK = 1024
KEY_ROWS = 256
VMEM_BYTES = 62 * 2**20


def dot(a, b):
    return jnp.dot(a, b, preferred_element_type=F32)


def rows_of(index, size):
    return pl.ds(pl.multiple_of(index * size, size), size)


def fold(x, op):
    return op(x.reshape(x.shape[0] // 8, 8, x.shape[1]), axis=0)


def ctx_peer(me, step):
    x = (me + step) % 4
    y = (me // 4 + step // 4) % 4
    z = (me // 16 + step // 16) % 2
    return z * 16 + y * 4 + x


def greet(devices):
    barrier = pltpu.get_barrier_semaphore()

    def signal(step, carry):
        peer = ctx_peer(lax.axis_index("ctx"), step)
        pl.semaphore_signal(barrier, inc=1, device_id={"ctx": peer}, device_id_type=MESH)
        return carry

    lax.fori_loop(1, devices, signal, 0)
    return barrier


def gather_heads_kernel(devices, q, k, v, og, ig, gm, qh, kh, vh, gfh, igh, gf, send_sem, recv_sem, own_sem):
    me = lax.axis_index("ctx")
    local = q.shape[0]
    barrier = greet(devices)

    def gate(index, carry):
        at = rows_of(index, LANES)
        gf[:, at] = (gm[:, at].astype(F32) * og[:, at].astype(F32)).astype(BF16)
        return carry

    lax.fori_loop(0, devices, gate, 0)
    pl.semaphore_wait(barrier, devices - 1)
    pairs = ((q, qh), (k, kh), (v, vh), (ig, igh), (gf, gfh))
    mine = rows_of(me, local)
    own = [
        pltpu.make_async_copy(src.at[:, rows_of(me, LANES)], dst.at[mine, :], own_sem.at[n])
        for n, (src, dst) in enumerate(pairs)
    ]
    for n, (src, dst) in enumerate(pairs):

        def send(step, carry, n=n, src=src, dst=dst):
            peer = ctx_peer(me, step)
            pltpu.make_async_remote_copy(
                src_ref=src.at[:, rows_of(peer, LANES)],
                dst_ref=dst.at[mine, :],
                send_sem=send_sem.at[n],
                recv_sem=recv_sem.at[n],
                device_id={"ctx": peer},
                device_id_type=MESH,
            ).start()
            return carry

        lax.fori_loop(1, devices, send, 0)
    for copy in own:
        copy.start()
    for n, (_, dst) in enumerate(pairs):
        own[n].wait()
        others = dst.at[pl.ds(0, (devices - 1) * local), :]
        pltpu.make_async_copy(others, others, recv_sem.at[n]).wait()
        pltpu.make_async_copy(others, others, send_sem.at[n]).wait()


def gather_heads(devices, q, k, v, og, ig, gm):
    local, channels = q.shape
    hbm = pl.BlockSpec(memory_space=pl.ANY)
    vmem = pl.BlockSpec(memory_space=pltpu.VMEM)
    head = jax.ShapeDtypeStruct((local * devices, LANES), BF16)
    return pl.pallas_call(
        functools.partial(gather_heads_kernel, devices),
        out_shape=(head,) * 5,
        in_specs=[hbm, hbm, hbm, vmem, hbm, vmem],
        out_specs=(hbm,) * 5,
        scratch_shapes=[pltpu.VMEM((local, channels), BF16)] + [pltpu.SemaphoreType.DMA((5,))] * 3,
        compiler_params=pltpu.CompilerParams(collective_id=0, has_side_effects=True),
        name="gather_heads",
    )(q, k, v, og, ig, gm)


def scatter_heads_kernel(devices, parts, *refs):
    sources, partial = refs[:5], refs[5]
    targets, partials = refs[6:11], refs[11]
    send_sem, recv_sem, own_sem, send_small, recv_small, own_small = refs[12:]
    me, part = lax.axis_index("ctx"), lax.axis_index("dp")
    local = targets[0].shape[0]
    few = partial.shape[0]
    barrier = pltpu.get_barrier_semaphore()

    def signal(step, carry):
        peer = ctx_peer(me, step // parts)
        other = (part + step) % parts
        pl.semaphore_signal(barrier, inc=1, device_id={"ctx": peer, "dp": other}, device_id_type=MESH)
        return carry

    lax.fori_loop(1, devices * parts, signal, 0)
    pl.semaphore_wait(barrier, devices * parts - 1)
    mine = rows_of(me, LANES)
    small = partials.at[rows_of(part * devices + me, few), :]

    def send_partial(step, carry):
        peer = ctx_peer(me, step // parts)
        other = (part + step) % parts
        pltpu.make_async_remote_copy(
            src_ref=partial,
            dst_ref=small,
            send_sem=send_small,
            recv_sem=recv_small,
            device_id={"ctx": peer, "dp": other},
            device_id_type=MESH,
        ).start()
        return carry

    lax.fori_loop(1, devices * parts, send_partial, 0)
    own = [
        pltpu.make_async_copy(src.at[rows_of(me, local), :], dst.at[:, mine], own_sem.at[n])
        for n, (src, dst) in enumerate(zip(sources, targets))
    ]
    for n, (src, dst) in enumerate(zip(sources, targets)):

        def send(step, carry, n=n, src=src, dst=dst):
            peer = ctx_peer(me, step)
            pltpu.make_async_remote_copy(
                src_ref=src.at[rows_of(peer, local), :],
                dst_ref=dst.at[:, mine],
                send_sem=send_sem.at[n],
                recv_sem=recv_sem.at[n],
                device_id={"ctx": peer},
                device_id_type=MESH,
            ).start()
            return carry

        lax.fori_loop(1, devices, send, 0)
    for copy in own:
        copy.start()
    own_part = pltpu.make_async_copy(partial, small, own_small)
    own_part.start()
    for n, dst in enumerate(targets):
        own[n].wait()
        others = dst.at[:, pl.ds(0, (devices - 1) * LANES)]
        pltpu.make_async_copy(others, others, recv_sem.at[n]).wait()
        pltpu.make_async_copy(others, others, send_sem.at[n]).wait()
    own_part.wait()
    others = partials.at[pl.ds(0, (devices * parts - 1) * few), :]
    for sem in (recv_small, send_small):
        pltpu.make_async_copy(others, others, sem).wait()


def scatter_heads(devices, parts, arrays, partial):
    tokens, width = arrays[0].shape
    hbm = pl.BlockSpec(memory_space=pl.ANY)
    rows = jax.ShapeDtypeStruct((tokens // devices, width * devices), BF16)
    few = partial.shape[0]
    return pl.pallas_call(
        functools.partial(scatter_heads_kernel, devices, parts),
        out_shape=(rows,) * 5 + (jax.ShapeDtypeStruct((parts * devices * few, partial.shape[1]), F32),),
        in_specs=[hbm] * 6,
        out_specs=(hbm,) * 6,
        scratch_shapes=[pltpu.SemaphoreType.DMA((5,))] * 3 + [pltpu.SemaphoreType.DMA] * 3,
        compiler_params=pltpu.CompilerParams(collective_id=1, has_side_effects=True),
        name="scatter_heads",
    )(*arrays, partial)


def head_kernel(
    groups, q, k, v, gf, ig, w,
    dq, dk, dv, gi, fil, gw,
    wf, gfp, xp, g, gg, later, earlier, kt, vt, s_all, dp_all, dka, dva, ot, dqt, corr,
):
    tokens, width = q.shape
    tile = later.shape[1] // 2
    per = width // groups
    block, part = QUERY_BLOCK, KEY_ROWS
    blocks = tokens // block
    pieces = block // part
    scale = width**-0.5
    factor = scale * math.log2(math.e)
    head = lax.axis_index("ctx")

    wf[...] = w[...].astype(F32)
    taps = wf[rows_of(head, groups), :]
    row = lax.broadcasted_iota(jnp.int32, (tile, tile), 0)
    col = lax.broadcasted_iota(jnp.int32, (tile, tile), 1)
    for n in range(groups):
        ring = jnp.broadcast_to(taps[n : n + 1, :], (tile, tile))
        shift = 1
        while shift < tile:
            ring = jnp.where((row & shift) != 0, pltpu.roll(ring, shift, 1), ring)
            shift *= 2
        upper = jnp.where(col >= row, ring, 0.0)
        lower = jnp.where(col < row, ring, 0.0)
        at = pl.ds(n * tile, tile)
        later[at, :tile] = upper.astype(BF16)
        later[at, tile:] = lower.astype(BF16)
        earlier[at, :tile] = lower.T.astype(BF16)
        earlier[at, tile:] = upper.T.astype(BF16)
    gfp[:tokens, :] = gf[...]
    gfp[tokens:, :] = jnp.zeros((tile, width), BF16)
    xp[:tile, :] = jnp.zeros((tile, width), BF16)

    lane_group = lax.broadcasted_iota(jnp.int32, (tile, width), 1) // per

    def convolved(matrix, signal, first):
        window = jnp.concatenate(
            [signal[pl.ds(pl.multiple_of(first + n * tile, tile), 2 * tile), :] for n in range(2)],
            axis=1,
        )
        result = [jnp.zeros((tile, width), F32)] * 2
        for n in range(groups):
            product = dot(matrix[pl.ds(n * tile, tile), :], window)
            for m in range(2):
                result[m] = jnp.where(lane_group == n, product[:, m * width : (m + 1) * width], result[m])
        return result

    def conv_back(index, carry):
        for m, value in enumerate(convolved(later, gfp, index * 2 * tile)):
            at = pl.ds(pl.multiple_of(index * 2 * tile + m * tile, tile), tile)
            gg[at, :] = value
            g[at, :] = (value * ig[at, :].astype(F32)).astype(BF16)
        return carry

    lax.fori_loop(0, tokens // (2 * tile), conv_back, 0)

    def turn(index, carry):
        at = rows_of(index, part)
        kt[index] = k[at, :].T
        vt[index] = v[at, :].T
        return carry

    lax.fori_loop(0, tokens // part, turn, 0)

    def query_block(i, carry):
        rows = rows_of(i, block)
        qb, gb = q[rows, :], g[rows, :]
        q_t, g_t = qb.T, gb.T

        def key_rows(j, r):
            return pl.ds(pl.multiple_of(j * block + r * part, part), part)

        def widen(value, skip, fill):
            if skip == 0:
                return value
            return jnp.concatenate([jnp.full((value.shape[0], skip), fill, F32), value], axis=1)

        def scores(j, top, diagonal=False):
            for r in range(pieces):
                at = key_rows(j, r)
                skip = r * part if diagonal else 0
                s = dot(k[at, :], q_t[:, skip:])
                if diagonal:
                    key_id = lax.broadcasted_iota(jnp.int32, s.shape, 0)
                    query_id = lax.broadcasted_iota(jnp.int32, s.shape, 1)
                    s = jnp.where(key_id <= query_id, s, -jnp.inf)
                s_all[at, skip:] = s
                top = jnp.maximum(top, widen(fold(s, jnp.max), skip, -jnp.inf))
            return top

        top = lax.fori_loop(0, i, scores, jnp.full((8, block), -jnp.inf, F32))
        top = jnp.max(scores(i, top, True), axis=0, keepdims=True)

        def probs(j, sums, diagonal=False):
            total, inner = sums
            for r in range(pieces):
                at = key_rows(j, r)
                skip = r * part if diagonal else 0
                p = jnp.exp2((s_all[at, skip:] - top[:, skip:]) * factor)
                grad_p = dot(v[at, :], g_t[:, skip:])
                s_all[at, skip:] = p
                dp_all[at, skip:] = grad_p
                total = total + widen(fold(p, jnp.sum), skip, 0.0)
                inner = inner + widen(fold(p * grad_p, jnp.sum), skip, 0.0)
            return total, inner

        none = jnp.zeros((8, block), F32)
        total, inner = probs(i, lax.fori_loop(0, i, probs, (none, none)), True)
        inverse = 1.0 / jnp.sum(total, axis=0, keepdims=True)
        inner = jnp.sum(inner, axis=0, keepdims=True) * inverse

        def grads(j, nothing, diagonal=False):
            for r in range(pieces):
                at = key_rows(j, r)
                skip = r * part if diagonal else 0
                p = s_all[at, skip:] * inverse[:, skip:]
                low = p.astype(BF16)
                grad_s = (p * (dp_all[at, skip:] - inner[:, skip:])).astype(BF16)
                value_part = dot(low, gb[skip:, :])
                key_part = dot(grad_s, qb[skip:, :])
                out_part = dot(vt[j * pieces + r], low)
                query_part = dot(kt[j * pieces + r], grad_s)
                if diagonal:
                    dva[at, :] = value_part
                    dka[at, :] = key_part
                else:
                    dva[at, :] += value_part
                    dka[at, :] += key_part
                if diagonal and r == 0:
                    ot[...] = out_part
                    dqt[...] = query_part
                else:
                    ot[:, skip:] += out_part
                    dqt[:, skip:] += query_part
            return nothing

        grads(i, 0, True)
        lax.fori_loop(0, i, grads, 0)
        attended = ot[...].T.astype(BF16).astype(F32)
        dq[rows, :] = (dqt[...] * scale).T.astype(BF16)
        gi[rows, :] = (gg[rows, :] * attended).astype(BF16)
        xp[pl.ds(pl.multiple_of(i * block + tile, tile), block), :] = (
            attended * ig[rows, :].astype(F32)
        ).astype(BF16)
        return carry

    lax.fori_loop(0, blocks, query_block, 0)

    def finish(index, carry):
        at = rows_of(index, part)
        dk[at, :] = (dka[at, :] * scale).astype(BF16)
        dv[at, :] = dva[at, :].astype(BF16)
        return carry

    lax.fori_loop(0, tokens // part, finish, 0)

    row_group = lax.broadcasted_iota(jnp.int32, (width, tile), 0) // per
    corr[...] = jnp.zeros_like(corr)

    def conv_ahead(index, carry):
        for m, value in enumerate(convolved(earlier, xp, index * 2 * tile)):
            at = pl.ds(pl.multiple_of(index * 2 * tile + m * tile, tile), tile)
            fil[at, :] = value.astype(BF16)
        lefts, rights = [], []
        for m in range(2):
            first = pl.multiple_of(index * 2 * tile + m * tile, tile)
            lefts.append(xp[pl.ds(first, 2 * tile), :])
            turned = gfp[pl.ds(first, tile), :].astype(F32).T
            rights.append(
                jnp.concatenate([jnp.where(row_group == n, turned, 0.0) for n in range(groups)], axis=1)
            )
        left = jnp.concatenate(lefts, axis=1)
        right = jnp.concatenate(rights, axis=0).astype(BF16)
        corr[...] += dot(left, right)
        return carry

    lax.fori_loop(0, tokens // (2 * tile), conv_ahead, 0)

    for n in range(groups):
        at = pl.ds(n * tile, tile)
        skewed = jnp.where(col >= row, corr[tile:, at], corr[:tile, at])
        shift = 1
        while shift < tile:
            skewed = jnp.where((row & shift) != 0, pltpu.roll(skewed, tile - shift, 1), skewed)
            shift *= 2
        gw[n : n + 1, :] = jnp.sum(skewed, axis=0, keepdims=True)


def one_head(q, k, v, gf, ig, w, devices):
    tokens, width = q.shape
    groups = w.shape[0] // devices
    tile = w.shape[1]
    head = jax.ShapeDtypeStruct((tokens, width), BF16)
    vmem = pl.BlockSpec(memory_space=pltpu.VMEM)
    part = KEY_ROWS
    return pl.pallas_call(
        functools.partial(head_kernel, groups),
        out_shape=(head,) * 5 + (jax.ShapeDtypeStruct((groups, tile), F32),),
        in_specs=[vmem] * 6,
        out_specs=(vmem,) * 6,
        scratch_shapes=[
            pltpu.VMEM(w.shape, F32),
            pltpu.VMEM((tokens + tile, width), BF16),
            pltpu.VMEM((tokens + tile, width), BF16),
            pltpu.VMEM((tokens, width), BF16),
            pltpu.VMEM((tokens, width), F32),
            pltpu.VMEM((groups * tile, 2 * tile), BF16),
            pltpu.VMEM((groups * tile, 2 * tile), BF16),
            pltpu.VMEM((tokens // part, width, part), BF16),
            pltpu.VMEM((tokens // part, width, part), BF16),
            pltpu.VMEM((tokens, QUERY_BLOCK), F32),
            pltpu.VMEM((tokens, QUERY_BLOCK), F32),
            pltpu.VMEM((tokens, width), F32),
            pltpu.VMEM((tokens, width), F32),
            pltpu.VMEM((width, QUERY_BLOCK), F32),
            pltpu.VMEM((width, QUERY_BLOCK), F32),
            pltpu.VMEM((2 * tile, groups * tile), F32),
        ],
        compiler_params=pltpu.CompilerParams(vmem_limit_bytes=VMEM_BYTES),
        name="one_head",
    )(q, k, v, gf, ig, w)


def results_kernel(
    dq, dk, dv, gi, fil, parts, og, gm, out_block, out_q, out_k, out_v, out_outer, out_inner, out_w
):
    filtered = fil[...].astype(F32)
    out_block[...] = (og[...].astype(F32) * filtered).astype(BF16)
    out_outer[...] = (gm[...].astype(F32) * filtered).astype(BF16)
    out_q[...] = dq[...]
    out_k[...] = dk[...]
    out_v[...] = dv[...]
    out_inner[...] = gi[...]
    out_w[...] = jnp.sum(parts[...], axis=0)


def results(arrays, partials, og, gm):
    rows, channels = og.shape
    steps = 4
    wide = pl.BlockSpec((rows // steps, channels), lambda i: (i, 0))
    n_parts, few, taps = partials.shape
    array = jax.ShapeDtypeStruct((rows, channels), BF16)
    return pl.pallas_call(
        results_kernel,
        grid=(steps,),
        out_shape=(array,) * 6 + (jax.ShapeDtypeStruct((few, taps), F32),),
        in_specs=[wide] * 5
        + [pl.BlockSpec((n_parts, few // steps, taps), lambda i: (0, i, 0))]
        + [wide] * 2,
        out_specs=(wide,) * 6 + (pl.BlockSpec((few // steps, taps), lambda i: (i, 0)),),
        name="results",
    )(*arrays, partials, og, gm)


def on_device(queries, attn_keys, attn_values, outer_gate, inner_gate, conv_filter, grad_mixed):
    devices, parts = lax.axis_size("ctx"), lax.axis_size("dp")
    og, gm = outer_gate[0], grad_mixed[0]
    heads = gather_heads(devices, queries[0], attn_keys[0], attn_values[0], og, inner_gate[0], gm)
    qh, kh, vh, gfh, igh = heads
    *arrays, partial = one_head(qh, kh, vh, gfh, igh, conv_filter, devices)
    *arrays, partials = scatter_heads(devices, parts, arrays, partial)
    partials = partials.reshape(parts, *conv_filter.shape)
    *arrays, grad_filter = results(arrays, partials, og, gm)
    return (*[array[None] for array in arrays], grad_filter)


def solution(mesh):
    spread = P("dp", "ctx", None)
    return jax.shard_map(
        on_device,
        mesh=mesh,
        in_specs=(spread,) * 5 + (P(), spread),
        out_specs=(spread,) * 6 + (P(),),
        check_vma=False,
    )
```

time: 739 us -> 215 us (0.29)
  Pallas kernels: 0 us -> 213 us
  matrix products: 211 us -> 0 us
  local copies, waits for them, and re-layouts: 159 us -> 0 us
  other arithmetic: 154 us -> 0 us
  waiting for transfers between devices: 128 us -> 0 us
  starting transfers between devices: 63.1 us -> 0 us
  between operations: 15.7 us -> 0.65 us
    pallas_call x0 -> x4, Pallas kernels: none -> 213 us  [the longest x1 81.8 us: scatter_heads(): pl.pallas_call(functools.partial(scatter_heads_kernel, devices, parts), o...]
    conv_general_dilated x3 -> x0, matrix products: 109 us -> none  [depthwise(): lax.conv_general_dilated(signal, taps[:, None, :], (1,), 'VALID', dimensi...]
    dot_general x48 -> x0, matrix products: 102 us -> none  [the longest x8 23 us: head_both(): jnp.einsum('qd,kd->qk', grad_block, value_rows[:last_row], preferred_elem...]
    psum x1 -> x0, waiting for transfers between devices: 99.2 us -> none  [on_device(): grad_filter = lax.psum(partial_grad, ('dp', 'ctx'))]
    unnamed x11 -> x0, other arithmetic: 91.7 us -> none
    all_to_all x8 -> x0, starting transfers between devices: 57.5 us -> none  [the longest x1 9.7 us: on_device(): lax.all_to_all(to_heads(attn_values), 'ctx', split_axis=2, concat_axis=1,...]
    another operation x4 -> x0, local copies, waits for them, and re-layouts: 53.3 us -> none  [token_major(): shaped.transpose(0, 2, 1, 3).reshape(batch_size, length, head_count * width)]
    unnamed x193 -> x0, local copies, waits for them, and re-layouts: 52.8 us -> none
  transfers between devices with their start and end apart: 11 -> 0, of which waited for: 5 -> 0; matrix products, arithmetic and copies ran while one was open for 31% -> 0% of each run, Pallas kernels for 0% -> 0%
where the time goes in v1:
time: 215 us; the launch traced here: 213 us
  Pallas kernels  213 us (99%)
    pallas_call x1, Pallas kernels, scatter_heads(): pl.pallas_call(functools.partial(scatter_heads_kernel, devices, parts), o...  81.8 us
    pallas_call x1, Pallas kernels, gather_heads(): pl.pallas_call(functools.partial(gather_heads_kernel, devices), out_shape...  72.8 us
    pallas_call x1, Pallas kernels, one_head(): pl.pallas_call(functools.partial(head_kernel, groups), out_shape=(head,)...  52.1 us
    pallas_call x1, Pallas kernels, results(): pl.pallas_call(results_kernel, grid=(steps,), out_shape=(array,) * 6 + (j...  6.13 us

profile of v1, /device:TPU:1, one launch (start us, length us, event | category | flops | bytes accessed | tf_op | source)
XLA Modules:
  0.0 213.4 jit_solution(3420237864189539409)
XLA Ops:
  0.6 72.8 %gather_heads.1 = (bf16[4096,128]{1,0:T(8,128)(2,1)}, bf16[4096,128]{1,0:T(8,128)(2,1)}, bf16[4096,128]{1,0:T(8,128)(2,1)}, bf16[4096,128]{1,0:T(8,128)(2,1)}, bf16[4096,128]{1,0:T(8,128)(2,1)}) custom-call(bf16[128,4096]{1,0:T(8,128)(2,1)} %bitcast.17, bf16[128,4096]{1,0:T(8,128)(2,1)} %bitcast.18, bf16[128,4096]{1,0:T(8,128)(2,1)} %bitcast.19, ...), custom_call_target="tpu_custom_call" | custom-call | tf_op jit(solution)/shard_map/gather_heads/pallas_call | solution.py:98
  73.5 52.1 %one_head.1 = (bf16[4096,128]{1,0:T(8,128)(2,1)}, bf16[4096,128]{1,0:T(8,128)(2,1)}, bf16[4096,128]{1,0:T(8,128)(2,1)}, bf16[4096,128]{1,0:T(8,128)(2,1)}, bf16[4096,128]{1,0:T(8,128)(2,1)}, /*index=5*/f32[8,128]{1,0:T(8,128)}) custom-call(bf16[4096,128]{1,0:T(8,128)(2,1)} %get-tuple-element.31.q, bf16[4096,128]{1,0:T(8,128)(2,1)} %get-tuple-element.32.k, ...), custom_call_target="tpu_custom_call" | custom-call | tf_op jit(solution)/shard_map/one_head/pallas_call | solution.py:391
  125.5 81.8 %scatter_heads.1 = (bf16[128,4096]{1,0:T(8,128)(2,1)}, bf16[128,4096]{1,0:T(8,128)(2,1)}, bf16[128,4096]{1,0:T(8,128)(2,1)}, bf16[128,4096]{1,0:T(8,128)(2,1)}, ...) custom-call(bf16[4096,128]{1,0:T(8,128)(2,1)} %get-tuple-element.36.refs_0_, bf16[4096,128]{1,0:T(8,128)(2,1)} %get-tuple-element.37.refs_1_, ...), custom_call_target="tpu_custom_call" | custom-call | tf_op jit(solution)/shard_map/scatter_heads/pallas_call | solution.py:182
  207.3 6.1 %results.1 = (bf16[128,4096]{1,0:T(8,128)(2,1)}, bf16[128,4096]{1,0:T(8,128)(2,1)}, bf16[128,4096]{1,0:T(8,128)(2,1)}, bf16[128,4096]{1,0:T(8,128)(2,1)}, bf16[1...) custom-call(bf16[128,4096]{1,0:T(8,128)(2,1)} %get-tuple-element.42.dq, ...), custom_call_target="tpu_custom_call" | custom-call | tf_op jit(solution)/shard_map/results/pallas_call | solution.py:438

commit v2 on v1

v2 whole, which is shorter than its diff:
```python
import functools
import math

import jax
import jax.numpy as jnp
from jax import lax
from jax.experimental import pallas as pl
from jax.experimental.pallas import tpu as pltpu
from jax.sharding import PartitionSpec as P

F32 = jnp.float32
BF16 = jnp.bfloat16
MESH = pl.DeviceIdType.MESH
LANES = 128
QUERY_BLOCK = 1024
KEY_ROWS = 256
VMEM_BYTES = 67_000_000


def dot(a, b):
    return jnp.dot(a, b, preferred_element_type=F32)


def rows_of(index, size):
    return pl.ds(pl.multiple_of(index * size, size), size)


def fold(x, op):
    return op(x.reshape(x.shape[0] // 8, 8, x.shape[1]), axis=0)


def ctx_peer(me, step):
    x = (me + step) % 4
    y = (me // 4 + step // 4) % 4
    z = (me // 16 + step // 16) % 2
    return z * 16 + y * 4 + x


def block_kernel(
    devices, parts, groups, q, k, v, ig, og, gm, w,
    dq_t, dk_t, dv_t, gi_t, fil_t, partials,
    qh, kh, vh, igh, gf, wf, gfp, xp, g, gg, later, earlier, kt, vt, s_all, dp_all, dka, dva, ot, dqt, corr,
    dq, gi, fil, gw,
    in_send, in_recv, in_own, out_send, out_recv, out_own, send_small, recv_small, own_small,
):
    me, part_id = lax.axis_index("ctx"), lax.axis_index("dp")
    local = q.shape[0]
    tokens, width = qh.shape
    tile = later.shape[1] // 2
    few = groups
    per = width // groups
    block, part = QUERY_BLOCK, KEY_ROWS
    blocks = tokens // block
    pieces = block // part
    targets = block // local
    scale = width**-0.5
    factor = scale * math.log2(math.e)

    barrier = pltpu.get_barrier_semaphore()

    def signal(step, carry):
        peer = ctx_peer(me, step // parts)
        other = (part_id + step) % parts
        pl.semaphore_signal(barrier, inc=1, device_id={"ctx": peer, "dp": other}, device_id_type=MESH)
        return carry

    lax.fori_loop(1, devices * parts, signal, 0)

    def gate(index, carry):
        at = rows_of(index, LANES)
        gf[:, at] = (gm[:, at].astype(F32) * og[:, at].astype(F32)).astype(BF16)
        return carry

    lax.fori_loop(0, devices, gate, 0)

    wf[...] = w[...].astype(F32)
    taps = wf[rows_of(me, groups), :]
    row = lax.broadcasted_iota(jnp.int32, (tile, tile), 0)
    col = lax.broadcasted_iota(jnp.int32, (tile, tile), 1)
    for n in range(groups):
        ring = jnp.broadcast_to(taps[n : n + 1, :], (tile, tile))
        shift = 1
        while shift < tile:
            ring = jnp.where((row & shift) != 0, pltpu.roll(ring, shift, 1), ring)
            shift *= 2
        upper = jnp.where(col >= row, ring, 0.0)
        lower = jnp.where(col < row, ring, 0.0)
        at = pl.ds(n * tile, tile)
        later[at, :tile] = upper.astype(BF16)
        later[at, tile:] = lower.astype(BF16)
        earlier[at, :tile] = lower.T.astype(BF16)
        earlier[at, tile:] = upper.T.astype(BF16)
    gfp[tokens:, :] = jnp.zeros((tile, width), BF16)
    xp[:tile, :] = jnp.zeros((tile, width), BF16)
    corr[...] = jnp.zeros_like(corr)

    pl.semaphore_wait(barrier, devices * parts - 1)

    mine = rows_of(me, local)
    incoming = ((gf, gfp), (ig, igh), (k, kh), (q, qh), (v, vh))
    for n, (src, dst) in enumerate(incoming):

        def send(step, carry, n=n, src=src, dst=dst):
            peer = ctx_peer(me, step)
            pltpu.make_async_remote_copy(
                src_ref=src.at[:, rows_of(peer, LANES)],
                dst_ref=dst.at[mine, :],
                send_sem=in_send.at[n],
                recv_sem=in_recv.at[n],
                device_id={"ctx": peer},
                device_id_type=MESH,
            ).start()
            return carry

        lax.fori_loop(1, devices, send, 0)
    own_in = [
        pltpu.make_async_copy(src.at[:, rows_of(me, LANES)], dst.at[mine, :], in_own.at[n])
        for n, (src, dst) in enumerate(incoming)
    ]
    for copy in own_in:
        copy.start()

    def arrived(n):
        own_in[n].wait()
        others = incoming[n][1].at[pl.ds(0, (devices - 1) * local), :]
        pltpu.make_async_copy(others, others, in_recv.at[n]).wait()

    lane_group = lax.broadcasted_iota(jnp.int32, (tile, width), 1) // per

    def convolved(matrix, signal, first):
        window = jnp.concatenate(
            [signal[pl.ds(pl.multiple_of(first + n * tile, tile), 2 * tile), :] for n in range(2)],
            axis=1,
        )
        result = [jnp.zeros((tile, width), F32)] * 2
        for n in range(groups):
            product = dot(matrix[pl.ds(n * tile, tile), :], window)
            for m in range(2):
                result[m] = jnp.where(lane_group == n, product[:, m * width : (m + 1) * width], result[m])
        return result

    def conv_back(index, carry):
        for m, value in enumerate(convolved(later, gfp, index * 2 * tile)):
            at = pl.ds(pl.multiple_of(index * 2 * tile + m * tile, tile), tile)
            gg[at, :] = value
            g[at, :] = (value * igh[at, :].astype(F32)).astype(BF16)
        return carry

    def turn(src, dst):
        def one(index, carry):
            dst[index] = src[rows_of(index, part), :].T
            return carry

        lax.fori_loop(0, tokens // part, one, 0)

    arrived(0)
    arrived(1)
    lax.fori_loop(0, tokens // (2 * tile), conv_back, 0)
    arrived(2)
    turn(kh, kt)
    arrived(3)

    row_group = lax.broadcasted_iota(jnp.int32, (width, tile), 0) // per

    def conv_ahead(index, carry):
        for m, value in enumerate(convolved(earlier, xp, index * 2 * tile)):
            at = pl.ds(pl.multiple_of(index * 2 * tile + m * tile, tile), tile)
            fil[at, :] = value.astype(BF16)
        lefts, rights = [], []
        for m in range(2):
            first = pl.multiple_of(index * 2 * tile + m * tile, tile)
            lefts.append(xp[pl.ds(first, 2 * tile), :])
            turned = gfp[pl.ds(first, tile), :].astype(F32).T
            rights.append(
                jnp.concatenate([jnp.where(row_group == n, turned, 0.0) for n in range(groups)], axis=1)
            )
        left = jnp.concatenate(lefts, axis=1)
        right = jnp.concatenate(rights, axis=0).astype(BF16)
        corr[...] += dot(left, right)
        return carry

    def conv_ahead_block(i):
        steps = block // (2 * tile)
        lax.fori_loop(i * steps, (i + 1) * steps, conv_ahead, 0)

    outgoing = ((dq, dq_t), (gi, gi_t), (fil, fil_t), (kh, dk_t), (vh, dv_t))
    columns = rows_of(me, LANES)

    def send_block(n, i):
        src, dst = outgoing[n]

        def one(step, carry):
            peer = i * targets + (me + step) % targets

            @pl.when(peer != me)
            def _():
                pltpu.make_async_remote_copy(
                    src_ref=src.at[rows_of(peer, local), :],
                    dst_ref=dst.at[:, columns],
                    send_sem=out_send.at[n],
                    recv_sem=out_recv.at[n],
                    device_id={"ctx": peer},
                    device_id_type=MESH,
                ).start()

            return carry

        lax.fori_loop(0, targets, one, 0)

    def send_all(n):
        src, dst = outgoing[n]

        def one(step, carry):
            peer = ctx_peer(me, step)
            pltpu.make_async_remote_copy(
                src_ref=src.at[rows_of(peer, local), :],
                dst_ref=dst.at[:, columns],
                send_sem=out_send.at[n],
                recv_sem=out_recv.at[n],
                device_id={"ctx": peer},
                device_id_type=MESH,
            ).start()
            return carry

        lax.fori_loop(1, devices, one, 0)

    def query_block(turn_id, carry):
        i = (me + turn_id) % blocks
        rows = rows_of(i, block)
        qb, gb = qh[rows, :], g[rows, :]
        q_t, g_t = qb.T, gb.T

        def key_rows(j, r):
            return pl.ds(pl.multiple_of(j * block + r * part, part), part)

        def widen(value, skip, fill):
            if skip == 0:
                return value
            return jnp.concatenate([jnp.full((value.shape[0], skip), fill, F32), value], axis=1)

        def scores(j, top, diagonal=False):
            for r in range(pieces):
                at = key_rows(j, r)
                skip = r * part if diagonal else 0
                s = dot(kh[at, :], q_t[:, skip:])
                if diagonal:
                    key_id = lax.broadcasted_iota(jnp.int32, s.shape, 0)
                    query_id = lax.broadcasted_iota(jnp.int32, s.shape, 1)
                    s = jnp.where(key_id <= query_id, s, -jnp.inf)
                s_all[at, skip:] = s
                top = jnp.maximum(top, widen(fold(s, jnp.max), skip, -jnp.inf))
            return top

        top = lax.fori_loop(0, i, scores, jnp.full((8, block), -jnp.inf, F32))
        top = jnp.max(scores(i, top, True), axis=0, keepdims=True)

        @pl.when(turn_id == 0)
        def _():
            arrived(4)
            turn(vh, vt)

        @pl.when(turn_id > 0)
        def _():
            before = (me + turn_id - 1) % blocks
            send_block(0, before)
            send_block(1, before)

        @pl.when(turn_id > 1)
        def _():
            send_block(2, (me + turn_id - 1) % blocks)

        def probs(j, sums, diagonal=False):
            total, inner = sums
            for r in range(pieces):
                at = key_rows(j, r)
                skip = r * part if diagonal else 0
                p = jnp.exp2((s_all[at, skip:] - top[:, skip:]) * factor)
                grad_p = dot(vh[at, :], g_t[:, skip:])
                s_all[at, skip:] = p
                dp_all[at, skip:] = grad_p
                total = total + widen(fold(p, jnp.sum), skip, 0.0)
                inner = inner + widen(fold(p * grad_p, jnp.sum), skip, 0.0)
            return total, inner

        none = jnp.zeros((8, block), F32)
        total, inner = probs(i, lax.fori_loop(0, i, probs, (none, none)), True)
        inverse = 1.0 / jnp.sum(total, axis=0, keepdims=True)
        inner = jnp.sum(inner, axis=0, keepdims=True) * inverse

        def grads(j, nothing, diagonal=False):
            for r in range(pieces):
                at = key_rows(j, r)
                skip = r * part if diagonal else 0
                p = s_all[at, skip:] * inverse[:, skip:]
                low = p.astype(BF16)
                grad_s = (p * (dp_all[at, skip:] - inner[:, skip:])).astype(BF16)
                dva[at, :] += dot(low, gb[skip:, :])
                dka[at, :] += dot(grad_s, qb[skip:, :])
                out_part = dot(vt[j * pieces + r], low)
                query_part = dot(kt[j * pieces + r], grad_s)
                if diagonal and r == 0:
                    ot[...] = out_part
                    dqt[...] = query_part
                else:
                    ot[:, skip:] += out_part
                    dqt[:, skip:] += query_part
            return nothing

        grads(i, 0, True)
        lax.fori_loop(0, i, grads, 0)
        attended = ot[...].T.astype(BF16).astype(F32)
        dq[rows, :] = (dqt[...] * scale).T.astype(BF16)
        gi[rows, :] = (gg[rows, :] * attended).astype(BF16)
        xp[pl.ds(pl.multiple_of(i * block + tile, tile), block), :] = (
            attended * igh[rows, :].astype(F32)
        ).astype(BF16)

        @pl.when(turn_id > 0)
        def _():
            conv_ahead_block(i)

        return carry

    dka[...] = jnp.zeros_like(dka)
    dva[...] = jnp.zeros_like(dva)
    lax.fori_loop(0, blocks, query_block, 0)

    def finish(index, carry):
        at = rows_of(index, part)
        kh[at, :] = (dka[at, :] * scale).astype(BF16)
        vh[at, :] = dva[at, :].astype(BF16)
        return carry

    lax.fori_loop(0, tokens // part, finish, 0)
    first_block, last_block = me % blocks, (me + blocks - 1) % blocks
    for n in range(3):
        send_block(n, last_block)
    send_all(3)
    send_all(4)
    conv_ahead_block(first_block)
    for n in range(groups):
        at = pl.ds(n * tile, tile)
        skewed = jnp.where(col >= row, corr[tile:, at], corr[:tile, at])
        shift = 1
        while shift < tile:
            skewed = jnp.where((row & shift) != 0, pltpu.roll(skewed, tile - shift, 1), skewed)
            shift *= 2
        gw[n : n + 1, :] = jnp.sum(skewed, axis=0, keepdims=True)
    send_block(2, first_block)

    small = partials.at[rows_of(part_id * devices + me, few), :]

    def send_partial(step, carry):
        peer = ctx_peer(me, step // parts)
        other = (part_id + step) % parts
        pltpu.make_async_remote_copy(
            src_ref=gw,
            dst_ref=small,
            send_sem=send_small,
            recv_sem=recv_small,
            device_id={"ctx": peer, "dp": other},
            device_id_type=MESH,
        ).start()
        return carry

    lax.fori_loop(1, devices * parts, send_partial, 0)
    own_part = pltpu.make_async_copy(gw, small, own_small)
    own_part.start()
    own_out = [
        pltpu.make_async_copy(src.at[mine, :], dst.at[:, columns], out_own.at[n])
        for n, (src, dst) in enumerate(outgoing)
    ]
    for copy in own_out:
        copy.start()
    for copy in own_out:
        copy.wait()
    own_part.wait()
    for n, (_, dst) in enumerate(outgoing):
        others = dst.at[:, pl.ds(0, (devices - 1) * LANES)]
        pltpu.make_async_copy(others, others, out_recv.at[n]).wait()
        pltpu.make_async_copy(others, others, out_send.at[n]).wait()
    for n, (_, dst) in enumerate(incoming):
        others = dst.at[pl.ds(0, (devices - 1) * local), :]
        pltpu.make_async_copy(others, others, in_send.at[n]).wait()
    others = partials.at[pl.ds(0, (devices * parts - 1) * few), :]
    for sem in (recv_small, send_small):
        pltpu.make_async_copy(others, others, sem).wait()


def block(devices, parts, q, k, v, ig, og, gm, w):
    local, channels = q.shape
    tokens, width = local * devices, channels // devices
    groups, tile = w.shape[0] // devices, w.shape[1]
    part = KEY_ROWS
    hbm = pl.BlockSpec(memory_space=pl.ANY)
    vmem = pl.BlockSpec(memory_space=pltpu.VMEM)
    rows = jax.ShapeDtypeStruct((local, channels), BF16)
    head = pltpu.VMEM((tokens, width), BF16)
    padded = pltpu.VMEM((tokens + tile, width), BF16)
    wide = pltpu.VMEM((tokens, width), F32)
    return pl.pallas_call(
        functools.partial(block_kernel, devices, parts, groups),
        out_shape=(rows,) * 5 + (jax.ShapeDtypeStruct((parts * w.shape[0], tile), F32),),
        in_specs=[hbm] * 4 + [vmem] * 3,
        out_specs=(hbm,) * 6,
        scratch_shapes=[
            head, head, head, head,
            pltpu.VMEM((local, channels), BF16),
            pltpu.VMEM(w.shape, F32),
            padded, padded, head, wide,
            pltpu.VMEM((groups * tile, 2 * tile), BF16),
            pltpu.VMEM((groups * tile, 2 * tile), BF16),
            pltpu.VMEM((tokens // part, width, part), BF16),
            pltpu.VMEM((tokens // part, width, part), BF16),
            pltpu.VMEM((tokens, QUERY_BLOCK), F32),
            pltpu.VMEM((tokens, QUERY_BLOCK), F32),
            wide, wide,
            pltpu.VMEM((width, QUERY_BLOCK), F32),
            pltpu.VMEM((width, QUERY_BLOCK), F32),
            pltpu.VMEM((2 * tile, groups * tile), F32),
            head, head, head,
            pltpu.VMEM((groups, tile), F32),
        ]
        + [pltpu.SemaphoreType.DMA((5,))] * 6
        + [pltpu.SemaphoreType.DMA] * 3,
        compiler_params=pltpu.CompilerParams(
            collective_id=0, has_side_effects=True, vmem_limit_bytes=VMEM_BYTES
        ),
        name="block",
    )(q, k, v, ig, og, gm, w)


def results_kernel(
    dq, dk, dv, gi, fil, parts, og, gm, out_block, out_q, out_k, out_v, out_outer, out_inner, out_w
):
    filtered = fil[...].astype(F32)
    out_block[...] = (og[...].astype(F32) * filtered).astype(BF16)
    out_outer[...] = (gm[...].astype(F32) * filtered).astype(BF16)
    out_q[...] = dq[...]
    out_k[...] = dk[...]
    out_v[...] = dv[...]
    out_inner[...] = gi[...]
    out_w[...] = jnp.sum(parts[...], axis=0)


def results(arrays, partials, og, gm):
    rows, channels = og.shape
    steps = 4
    wide = pl.BlockSpec((rows // steps, channels), lambda i: (i, 0))
    n_parts, few, taps = partials.shape
    array = jax.ShapeDtypeStruct((rows, channels), BF16)
    return pl.pallas_call(
        results_kernel,
        grid=(steps,),
        out_shape=(array,) * 6 + (jax.ShapeDtypeStruct((few, taps), F32),),
        in_specs=[wide] * 5
        + [pl.BlockSpec((n_parts, few // steps, taps), lambda i: (0, i, 0))]
        + [wide] * 2,
        out_specs=(wide,) * 6 + (pl.BlockSpec((few // steps, taps), lambda i: (i, 0)),),
        name="results",
    )(*arrays, partials, og, gm)


def on_device(queries, attn_keys, attn_values, outer_gate, inner_gate, conv_filter, grad_mixed):
    devices, parts = lax.axis_size("ctx"), lax.axis_size("dp")
    og, gm = outer_gate[0], grad_mixed[0]
    *arrays, partials = block(
        devices, parts, queries[0], attn_keys[0], attn_values[0], inner_gate[0], og, gm, conv_filter
    )
    partials = partials.reshape(parts, *conv_filter.shape)
    dq, dk, dv, gi, fil = arrays
    *arrays, grad_filter = results((dq, dk, dv, gi, fil), partials, og, gm)
    return (*[array[None] for array in arrays], grad_filter)


def solution(mesh):
    spread = P("dp", "ctx", None)
    return jax.shard_map(
        on_device,
        mesh=mesh,
        in_specs=(spread,) * 5 + (P(), spread),
        out_specs=(spread,) * 6 + (P(),),
        check_vma=False,
    )
```

time: 215 us -> 173 us (0.80)
  Pallas kernels: 213 us -> 172 us
    pallas_call x3 -> x1, Pallas kernels: 207 us -> 166 us  [block(): pl.pallas_call(functools.partial(block_kernel, devices, parts, groups), o...]
where the time goes in v2:
time: 173 us
  Pallas kernels  172 us (99%)
    pallas_call x1, Pallas kernels, block(): pl.pallas_call(functools.partial(block_kernel, devices, parts, groups), o...  166 us
    pallas_call x1, Pallas kernels, results(): pl.pallas_call(results_kernel, grid=(steps,), out_shape=(array,) * 6 + (j...  6.13 us

profile of v2, /device:TPU:1, one launch (start us, length us, event | category | flops | bytes accessed | tf_op | source)
XLA Modules:
  0.0 172.8 jit_solution(11977505555440088084)
XLA Ops:
  0.6 166.1 %block.1 = (bf16[128,4096]{1,0:T(8,128)(2,1)}, bf16[128,4096]{1,0:T(8,128)(2,1)}, bf16[128,4096]{1,0:T(8,128)(2,1)}, bf16[128,4096]{1,0:T(8,128)(2,1)}, bf16[128,4096]{1,0:T(8,128)(2,1)}, /*index=5*/f32[1024,128]{1,0:T(8,128)}) custom-call(bf16[128,4096]{1,0:T(8,128)(2,1)} %bitcast.17, bf16[128,4096]{1,0:T(8,128)(2,1)} %bitcast.18, ...), custom_call_target="tpu_custom_call" | custom-call | tf_op jit(solution)/shard_map/block/pallas_call | solution.py:401
  166.7 6.1 %results.1 = (bf16[128,4096]{1,0:T(8,128)(2,1)}, bf16[128,4096]{1,0:T(8,128)(2,1)}, bf16[128,4096]{1,0:T(8,128)(2,1)}, bf16[128,4096]{1,0:T(8,128)(2,1)}, bf16[1...) custom-call(bf16[128,4096]{1,0:T(8,128)(2,1)} %get-tuple-element.20.dq, ...), custom_call_target="tpu_custom_call" | custom-call | tf_op jit(solution)/shard_map/results/pallas_call | solution.py:452

commit v3 on v2

--- a/solution.py
+++ b/solution.py
@@ -38,10 +38,10 @@
 
 def block_kernel(
     devices, parts, groups, q, k, v, ig, og, gm, w,
-    dq_t, dk_t, dv_t, gi_t, fil_t, partials,
+    dq_t, dk_t, dv_t, gi_t, fil_t, totals,
     qh, kh, vh, igh, gf, wf, gfp, xp, g, gg, later, earlier, kt, vt, s_all, dp_all, dka, dva, ot, dqt, corr,
-    dq, gi, fil, gw,
-    in_send, in_recv, in_own, out_send, out_recv, out_own, send_small, recv_small, own_small,
+    dq, gi, fil, gw, total_w,
+    in_send, in_recv, in_own, out_send, out_recv, out_own, send_small, recv_small, own_small, share_send, share_recv,
 ):
     me, part_id = lax.axis_index("ctx"), lax.axis_index("dp")
     local = q.shape[0]
@@ -59,12 +59,19 @@
     barrier = pltpu.get_barrier_semaphore()
 
     def signal(step, carry):
-        peer = ctx_peer(me, step // parts)
-        other = (part_id + step) % parts
-        pl.semaphore_signal(barrier, inc=1, device_id={"ctx": peer, "dp": other}, device_id_type=MESH)
-        return carry
-
-    lax.fori_loop(1, devices * parts, signal, 0)
+        pl.semaphore_signal(
+            barrier, inc=1, device_id={"ctx": ctx_peer(me, step)}, device_id_type=MESH
+        )
+        return carry
+
+    def signal_part(step, carry):
+        pl.semaphore_signal(
+            barrier, inc=1, device_id={"dp": (part_id + step) % parts}, device_id_type=MESH
+        )
+        return carry
+
+    lax.fori_loop(1, devices, signal, 0)
+    lax.fori_loop(1, parts, signal_part, 0)
 
     def gate(index, carry):
         at = rows_of(index, LANES)
@@ -72,6 +79,32 @@
         return carry
 
     lax.fori_loop(0, devices, gate, 0)
+
+    pl.semaphore_wait(barrier, devices + parts - 2)
+
+    mine = rows_of(me, local)
+    incoming = ((gf, gfp), (ig, igh), (k, kh), (q, qh), (v, vh))
+    for n, (src, dst) in enumerate(incoming):
+
+        def send(step, carry, n=n, src=src, dst=dst):
+            peer = ctx_peer(me, step)
+            pltpu.make_async_remote_copy(
+                src_ref=src.at[:, rows_of(peer, LANES)],
+                dst_ref=dst.at[mine, :],
+                send_sem=in_send.at[n],
+                recv_sem=in_recv.at[n],
+                device_id={"ctx": peer},
+                device_id_type=MESH,
+            ).start()
+            return carry
+
+        lax.fori_loop(1, devices, send, 0)
+    own_in = [
+        pltpu.make_async_copy(src.at[:, rows_of(me, LANES)], dst.at[mine, :], in_own.at[n])
+        for n, (src, dst) in enumerate(incoming)
+    ]
+    for copy in own_in:
+        copy.start()
 
     wf[...] = w[...].astype(F32)
     taps = wf[rows_of(me, groups), :]
@@ -94,31 +127,8 @@
     xp[:tile, :] = jnp.zeros((tile, width), BF16)
     corr[...] = jnp.zeros_like(corr)
 
-    pl.semaphore_wait(barrier, devices * parts - 1)
-
-    mine = rows_of(me, local)
-    incoming = ((gf, gfp), (ig, igh), (k, kh), (q, qh), (v, vh))
-    for n, (src, dst) in enumerate(incoming):
-
-        def send(step, carry, n=n, src=src, dst=dst):
-            peer = ctx_peer(me, step)
-            pltpu.make_async_remote_copy(
-                src_ref=src.at[:, rows_of(peer, LANES)],
-                dst_ref=dst.at[mine, :],
-                send_sem=in_send.at[n],
-                recv_sem=in_recv.at[n],
-                device_id={"ctx": peer},
-                device_id_type=MESH,
-            ).start()
-            return carry
-
-        lax.fori_loop(1, devices, send, 0)
-    own_in = [
-        pltpu.make_async_copy(src.at[:, rows_of(me, LANES)], dst.at[mine, :], in_own.at[n])
-        for n, (src, dst) in enumerate(incoming)
-    ]
-    for copy in own_in:
-        copy.start()
+    dka[...] = jnp.zeros_like(dka)
+    dva[...] = jnp.zeros_like(dva)
 
     def arrived(n):
         own_in[n].wait()
@@ -321,8 +331,6 @@
 
         return carry
 
-    dka[...] = jnp.zeros_like(dka)
-    dva[...] = jnp.zeros_like(dva)
     lax.fori_loop(0, blocks, query_block, 0)
 
     def finish(index, carry):
@@ -335,8 +343,6 @@
     first_block, last_block = me % blocks, (me + blocks - 1) % blocks
     for n in range(3):
         send_block(n, last_block)
-    send_all(3)
-    send_all(4)
     conv_ahead_block(first_block)
     for n in range(groups):
         at = pl.ds(n * tile, tile)
@@ -345,26 +351,41 @@
         while shift < tile:
             skewed = jnp.where((row & shift) != 0, pltpu.roll(skewed, tile - shift, 1), skewed)
             shift *= 2
-        gw[n : n + 1, :] = jnp.sum(skewed, axis=0, keepdims=True)
+        gw[part_id, n : n + 1, :] = jnp.sum(skewed, axis=0, keepdims=True)
+    send_all(3)
+
+    def share(step, carry):
+        pltpu.make_async_remote_copy(
+            src_ref=gw.at[part_id],
+            dst_ref=gw.at[part_id],
+            send_sem=share_send,
+            recv_sem=share_recv,
+            device_id={"dp": (part_id + step) % parts},
+            device_id_type=MESH,
+        ).start()
+        return carry
+
+    lax.fori_loop(1, parts, share, 0)
+    send_all(4)
     send_block(2, first_block)
-
-    small = partials.at[rows_of(part_id * devices + me, few), :]
-
-    def send_partial(step, carry):
-        peer = ctx_peer(me, step // parts)
-        other = (part_id + step) % parts
+    shared = gw.at[pl.ds(0, parts - 1)]
+    pltpu.make_async_copy(shared, shared, share_recv).wait()
+    total_w[...] = jnp.sum(gw[...], axis=0)
+    small = totals.at[rows_of(me, few), :]
+
+    def send_total(step, carry):
         pltpu.make_async_remote_copy(
-            src_ref=gw,
+            src_ref=total_w,
             dst_ref=small,
             send_sem=send_small,
             recv_sem=recv_small,
-            device_id={"ctx": peer, "dp": other},
+            device_id={"ctx": ctx_peer(me, step)},
             device_id_type=MESH,
         ).start()
         return carry
 
-    lax.fori_loop(1, devices * parts, send_partial, 0)
-    own_part = pltpu.make_async_copy(gw, small, own_small)
+    lax.fori_loop(1, devices, send_total, 0)
+    own_part = pltpu.make_async_copy(total_w, small, own_small)
     own_part.start()
     own_out = [
         pltpu.make_async_copy(src.at[mine, :], dst.at[:, columns], out_own.at[n])
@@ -382,7 +403,8 @@
     for n, (_, dst) in enumerate(incoming):
         others = dst.at[pl.ds(0, (devices - 1) * local), :]
         pltpu.make_async_copy(others, others, in_send.at[n]).wait()
-    others = partials.at[pl.ds(0, (devices * parts - 1) * few), :]
+    pltpu.make_async_copy(shared, shared, share_send).wait()
+    others = totals.at[pl.ds(0, (devices - 1) * few), :]
     for sem in (recv_small, send_small):
         pltpu.make_async_copy(others, others, sem).wait()
 
@@ -400,7 +422,7 @@
     wide = pltpu.VMEM((tokens, width), F32)
     return pl.pallas_call(
         functools.partial(block_kernel, devices, parts, groups),
-        out_shape=(rows,) * 5 + (jax.ShapeDtypeStruct((parts * w.shape[0], tile), F32),),
+        out_shape=(rows,) * 5 + (jax.ShapeDtypeStruct(w.shape, F32),),
         in_specs=[hbm] * 4 + [vmem] * 3,
         out_specs=(hbm,) * 6,
         scratch_shapes=[
@@ -419,10 +441,11 @@
             pltpu.VMEM((width, QUERY_BLOCK), F32),
             pltpu.VMEM((2 * tile, groups * tile), F32),
             head, head, head,
+            pltpu.VMEM((parts, groups, tile), F32),
             pltpu.VMEM((groups, tile), F32),
         ]
         + [pltpu.SemaphoreType.DMA((5,))] * 6
-        + [pltpu.SemaphoreType.DMA] * 3,
+        + [pltpu.SemaphoreType.DMA] * 5,
         compiler_params=pltpu.CompilerParams(
             collective_id=0, has_side_effects=True, vmem_limit_bytes=VMEM_BYTES
         ),
@@ -431,7 +454,7 @@
 
 
 def results_kernel(
-    dq, dk, dv, gi, fil, parts, og, gm, out_block, out_q, out_k, out_v, out_outer, out_inner, out_w
+    dq, dk, dv, gi, fil, totals, og, gm, out_block, out_q, out_k, out_v, out_outer, out_inner, out_w
 ):
     filtered = fil[...].astype(F32)
     out_block[...] = (og[...].astype(F32) * filtered).astype(BF16)
@@ -440,36 +463,35 @@
     out_k[...] = dk[...]
     out_v[...] = dv[...]
     out_inner[...] = gi[...]
-    out_w[...] = jnp.sum(parts[...], axis=0)
-
-
-def results(arrays, partials, og, gm):
+    out_w[...] = totals[...]
+
+
+def results(arrays, totals, og, gm):
     rows, channels = og.shape
     steps = 4
     wide = pl.BlockSpec((rows // steps, channels), lambda i: (i, 0))
-    n_parts, few, taps = partials.shape
+    few, taps = totals.shape
     array = jax.ShapeDtypeStruct((rows, channels), BF16)
     return pl.pallas_call(
         results_kernel,
         grid=(steps,),
         out_shape=(array,) * 6 + (jax.ShapeDtypeStruct((few, taps), F32),),
         in_specs=[wide] * 5
-        + [pl.BlockSpec((n_parts, few // steps, taps), lambda i: (0, i, 0))]
+        + [pl.BlockSpec((few // steps, taps), lambda i: (i, 0))]
         + [wide] * 2,
         out_specs=(wide,) * 6 + (pl.BlockSpec((few // steps, taps), lambda i: (i, 0)),),
         name="results",
-    )(*arrays, partials, og, gm)
+    )(*arrays, totals, og, gm)
 
 
 def on_device(queries, attn_keys, attn_values, outer_gate, inner_gate, conv_filter, grad_mixed):
     devices, parts = lax.axis_size("ctx"), lax.axis_size("dp")
     og, gm = outer_gate[0], grad_mixed[0]
-    *arrays, partials = block(
+    *arrays, totals = block(
         devices, parts, queries[0], attn_keys[0], attn_values[0], inner_gate[0], og, gm, conv_filter
     )
-    partials = partials.reshape(parts, *conv_filter.shape)
     dq, dk, dv, gi, fil = arrays
-    *arrays, grad_filter = results((dq, dk, dv, gi, fil), partials, og, gm)
+    *arrays, grad_filter = results((dq, dk, dv, gi, fil), totals, og, gm)
     return (*[array[None] for array in arrays], grad_filter)
 
 

time: 173 us -> 166 us (0.960)
  Pallas kernels: 172 us -> 165 us
    pallas_call x1, Pallas kernels: 166 us -> 159 us  [block(): pl.pallas_call(functools.partial(block_kernel, devices, parts, groups), o...]
where the time goes in v3:
time: 166 us
  Pallas kernels  165 us (99%)
    pallas_call x1, Pallas kernels, block(): pl.pallas_call(functools.partial(block_kernel, devices, parts, groups), o...  159 us
    pallas_call x1, Pallas kernels, results(): pl.pallas_call(results_kernel, grid=(steps,), out_shape=(array,) * 6 + (j...  6.07 us

profile of v3, /device:TPU:1, one launch (start us, length us, event | category | flops | bytes accessed | tf_op | source)
XLA Modules:
  0.0 165.7 jit_solution(4256857232343595501)
XLA Ops:
  0.6 159.0 %block.1 = (bf16[128,4096]{1,0:T(8,128)(2,1)}, bf16[128,4096]{1,0:T(8,128)(2,1)}, bf16[128,4096]{1,0:T(8,128)(2,1)}, bf16[128,4096]{1,0:T(8,128)(2,1)}, bf16[128,4096]{1,0:T(8,128)(2,1)}, /*index=5*/f32[256,128]{1,0:T(8,128)}) custom-call(bf16[128,4096]{1,0:T(8,128)(2,1)} %bitcast.16, bf16[128,4096]{1,0:T(8,128)(2,1)} %bitcast.17, ...), custom_call_target="tpu_custom_call" | custom-call | tf_op jit(solution)/shard_map/block/pallas_call | solution.py:423
  159.6 6.1 %results.1 = (bf16[128,4096]{1,0:T(8,128)(2,1)}, bf16[128,4096]{1,0:T(8,128)(2,1)}, bf16[128,4096]{1,0:T(8,128)(2,1)}, bf16[128,4096]{1,0:T(8,128)(2,1)}, bf16[1...) custom-call(bf16[128,4096]{1,0:T(8,128)(2,1)} %get-tuple-element.20.dq, ...), custom_call_target="tpu_custom_call" | custom-call | tf_op jit(solution)/shard_map/results/pallas_call | solution.py:475
